TPU v7x, 32 devices: a whole 2x2x4 slice. The times are simulated.
32 devices in a mesh: domain: 8 (over z, y), vec: 4 (over x, core).
Axes of the slice: x: 2, y: 2, z: 4, core: 2. Of those that a mesh axis runs over, the one named last changes fastest.
Arguments:
- vectors: float32 [4096, 512], P('domain', 'vec'), may hold values from -6 to 6
- hamiltonian: float32 [512, 128, 128], P('domain'), may hold values from -0.09375 to 0.09375
- tile_pairs: int32 [512, 2], P('domain'), may hold values from 0 to 31, as said below
- tile_counts: int32 [8], P('domain'), may hold values from 8 to 64, as said below
Outputs:
- filtered: float32 [4096, 512], P('domain', 'vec')
- gram: float32 [512, 512], P('vec')
Inputs may be any that keep to these rules, and one draw needn't show every extreme that they name: `tile_pairs`: slots k * 64 to (k + 1) * 64 - 1 have their row group r among groups k * 4 to (k + 1) * 4 - 1 and their column group c with r <= c <= min(k * 4 + 3 * 4 - 1, 31); pairs may repeat, and repeated blocks add. `tile_counts`: one domain index uses all 64 slots.
All inputs are finite; a program needn't handle non-finite values.
Results may differ from a plain program's by a relative error of at most 0.0003.
Values sent between devices are 32-bit elements; how exact they have to be, the bound alone decides.
A program may use at most 64 MiB of HBM per device.

v0:
```python
import jax
import jax.numpy as jnp
from jax import lax
from jax.sharding import PartitionSpec as P

TILE = 128
REACH = 2
center_shift = 1.0
half_width = 1.5


def from_behind(block, axis, distance):
    devices = range(lax.axis_size(axis))
    route = [(i - distance, i) for i in devices if i - distance in devices]
    return lax.ppermute(block, axis, route)


def local_products(own, window, tiles, row_loc, col_loc, count, groups):
    block_slots = 8
    width = own.shape[2]
    span = window.shape[0]
    n_blocks = (count + block_slots - 1) // block_slots

    def block_step(index, carry):
        rows_acc, back_acc = carry
        start = index * block_slots
        tile = lax.dynamic_slice_in_dim(tiles, start, block_slots, 0)
        rloc = lax.dynamic_slice_in_dim(row_loc, start, block_slots, 0)
        cloc = lax.dynamic_slice_in_dim(col_loc, start, block_slots, 0)
        used = (start + jnp.arange(block_slots, dtype=jnp.int32) < count).astype(jnp.float32)
        apart = (rloc != cloc).astype(jnp.float32)
        fwd = jnp.einsum("tij,tjc->tic", tile, window[cloc], precision=lax.Precision.HIGHEST)
        back = jnp.einsum("tji,tjc->tic", tile, own[rloc], precision=lax.Precision.HIGHEST)
        row_hot = (rloc[:, None] == jnp.arange(groups, dtype=jnp.int32)[None, :]).astype(
            jnp.float32
        ) * used[:, None]
        col_hot = (cloc[:, None] == jnp.arange(span, dtype=jnp.int32)[None, :]).astype(
            jnp.float32
        ) * (used * apart)[:, None]
        rows_acc = rows_acc + jnp.einsum(
            "tg,tic->gic", row_hot, fwd, precision=lax.Precision.HIGHEST
        )
        back_acc = back_acc + jnp.einsum(
            "tg,tic->gic", col_hot, back, precision=lax.Precision.HIGHEST
        )
        return (rows_acc, back_acc)

    start_rows = jnp.zeros((groups, TILE, width), jnp.float32)
    start_back = jnp.zeros((span, TILE, width), jnp.float32)
    return lax.fori_loop(0, n_blocks, block_step, (start_rows, start_back))


def apply_ham(block, tiles, row_loc, col_loc, count):
    groups = block.shape[0] // TILE
    width = block.shape[1]
    own = block.reshape(groups, TILE, width)
    pieces = [own]
    for step in range(1, REACH + 1):
        pieces.append(from_behind(own, "domain", -step))
    window = jnp.concatenate(pieces, 0)
    rows_acc, back_acc = local_products(own, window, tiles, row_loc, col_loc, count, groups)
    result = rows_acc + back_acc[:groups]
    for step in range(1, REACH + 1):
        result = result + from_behind(back_acc[step * groups : (step + 1) * groups], "domain", step)
    return result.reshape(groups * TILE, width)


def shards(vectors, hamiltonian, tile_pairs, tile_counts):
    groups = vectors.shape[0] // TILE
    base = lax.axis_index("domain") * groups
    count = tile_counts[0]
    diag = tile_pairs[:, 0] == tile_pairs[:, 1]
    tiles = jnp.where(
        diag[:, None, None], 0.5 * (hamiltonian + jnp.swapaxes(hamiltonian, 1, 2)), hamiltonian
    )
    row_loc = tile_pairs[:, 0] - base
    col_loc = tile_pairs[:, 1] - base
    second = (
        apply_ham(vectors, tiles, row_loc, col_loc, count) - center_shift * vectors
    ) / half_width
    third = (
        2.0
        * (apply_ham(second, tiles, row_loc, col_loc, count) - center_shift * second)
        / half_width
        - vectors
    )
    filtered = (
        2.0 * (apply_ham(third, tiles, row_loc, col_loc, count) - center_shift * third) / half_width
        - second
    )
    total_rows = vectors.shape[0] * lax.axis_size("domain")
    gathered = lax.all_gather(filtered, "vec", axis=1, tiled=True)
    partial_block = (
        jnp.dot(
            filtered.T,
            gathered,
            precision=lax.Precision.HIGHEST,
            preferred_element_type=jnp.float32,
        )
        / total_rows
    )
    gram = lax.psum(partial_block, "domain")
    return (filtered, gram)


def solution(mesh):
    in_specs = (P("domain", "vec"), P("domain", None, None), P("domain", None), P("domain"))
    out_specs = (P("domain", "vec"), P("vec", None))
    return jax.shard_map(shards, mesh=mesh, in_specs=in_specs, out_specs=out_specs, check_vma=False)
```

profile of v0, /device:TPU:0, one launch (start us, length us, event | category | flops | bytes accessed | tf_op | source)
XLA Modules:
  0.0 392.4 jit_solution(13187985193437510828)
XLA Ops:
  9.8 5.6 %copy.6 = f32[64,128,128]{1,2,0:T(8,128)} copy(f32[64,128,128]{2,1,0:T(8,128)} %param.11) | data formatting | bytes 8388608 | tf_op args[1]
  15.4 5.9 %fusion.61 = f32[64,128,128]{2,1,0:T(8,128)} fusion(f32[64,128,128]{2,1,0:T(8,128)} %param.11, f32[64,128,128]{1,2,0:T(8,128)} %copy.6, pred[64]{0:T(512)(128)(4,1)S(1)} %compare_bitcast_fusion), kind=kLoop, calls=%fused_computation.98 | loop fusion | flops 3145728 | bytes 12582976 | tf_op jit(solution)/shard_map/jit(_where)/select_n | solution.py:73
  22.3 24.5 %while.36 = (s32[]{:T(128)}, f32[4,128,128]{2,0,1:T(4,128)S(1)}, f32[12,128,128]{2,0,1:T(8,128)S(1)}, s32[]{:T(128)}, s32[64]{0:T(128)S(1)}, /*index=5*/s32[]{:T...) while((s32[]{:T(128)}, f32[4,128,128]{2,0,1:T(4,128)S(1)}, ...), condition=%wide.region_1.2_spmd, body=%wide.region_0.1_spmd.sunk | while | flops 428083552 | bytes 8397583 | solution.py:50
  26.9 2.1 fusion.117
  35.1 2.1 fusion.117
  43.2 2.1 fusion.117
  48.2 5.6 %collective-permute-start.2 = (f32[4,128,128]{2,0,1:T(4,128)S(1)}, f32[4,128,128]{2,0,1:T(4,128)S(1)}, u32[]{:S(2)}, u32[]{:S(2)}) collective-permute-start(f32[4,128,128]{2,0,1:T(4,128)S(1)} %get-tuple-element.252), channel_id=1, source_target_pairs={{0,4},{4,8},{8,12},{12,16},{16,20},{20,24},{24,28},{1,5},{5,9},{9,... | collective-permute-start | bytes 786440 | tf_op jit(solution)/shard_map/ppermute | solution.py:15
  54.7 4.6 %collective-permute-done.2 = f32[4,128,128]{2,0,1:T(4,128)S(1)} collective-permute-done((f32[4,128,128]{2,0,1:T(4,128)S(1)}, f32[4,128,128]{2,0,1:T(4,128)S(1)}, u32[]{:S(2)}, u32[]{:S(2)}) %collective-permute-start.2) | collective-permute-done | bytes 262176 | tf_op jit(solution)/shard_map/ppermute | solution.py:15
  62.1 51.8 %collective-permute-done.5 = f32[4,128,128]{2,1,0:T(8,128)S(1)} collective-permute-done((f32[4,128,128]{2,1,0:T(8,128)S(1)}, f32[4,128,128]{2,1,0:T(8,128)S(1)}, u32[]{:S(2)}, u32[]{:S(2)}) %collective-permute-start.5) | collective-permute-done | bytes 262176 | tf_op jit(solution)/shard_map/ppermute | solution.py:15
  114.1 24.5 %while.37 = (s32[]{:T(128)}, f32[4,128,128]{2,0,1:T(4,128)S(1)}, f32[12,128,128]{2,0,1:T(8,128)S(1)}, s32[]{:T(128)}, s32[64]{0:T(128)S(1)}, /*index=5*/s32[]{:T...) while((s32[]{:T(128)}, f32[4,128,128]{2,0,1:T(4,128)S(1)}, ...), condition=%wide.region_3.4_spmd, body=%wide.region_2.3_spmd.sunk | while | flops 428083552 | bytes 8397583 | solution.py:50
  118.7 2.1 fusion.127
  126.9 2.1 fusion.127
  135.0 2.1 fusion.127
  140.0 6.4 %collective-permute-start.6 = (f32[4,128,128]{2,0,1:T(4,128)S(1)}, f32[4,128,128]{2,0,1:T(4,128)S(1)}, u32[]{:S(2)}, u32[]{:S(2)}) collective-permute-start(f32[4,128,128]{2,0,1:T(4,128)S(1)} %get-tuple-element.250), channel_id=1, source_target_pairs={{0,4},{4,8},{8,12},{12,16},{16,20},{20,24},{24,28},{1,5},{5,9},{9,... | collective-permute-start | bytes 786440 | tf_op jit(solution)/shard_map/ppermute | solution.py:15
  146.5 3.8 collective-permute-done.6
  153.2 54.4 %collective-permute-done.9 = f32[4,128,128]{2,1,0:T(8,128)S(1)} collective-permute-done((f32[4,128,128]{2,1,0:T(8,128)S(1)}, f32[4,128,128]{2,1,0:T(8,128)S(1)}, u32[]{:S(2)}, u32[]{:S(2)}) %collective-permute-start.9) | collective-permute-done | bytes 262176 | tf_op jit(solution)/shard_map/ppermute | solution.py:15
  207.7 24.7 %while.38 = (s32[]{:T(128)}, f32[4,128,128]{2,0,1:T(4,128)S(1)}, f32[12,128,128]{2,0,1:T(8,128)S(1)}, s32[]{:T(128)}, s32[64]{0:T(128)S(1)}, /*index=5*/s32[]{:T...) while((s32[]{:T(128)}, f32[4,128,128]{2,0,1:T(4,128)S(1)}, ...), condition=%wide.region_5.6_spmd, body=%wide.region_4.5_spmd.sunk | while | flops 428083552 | bytes 8397583 | solution.py:50
  212.5 2.1 fusion.137
  220.7 2.1 fusion.137
  233.9 6.2 %collective-permute-start.10 = (f32[4,128,128]{2,0,1:T(4,128)S(1)}, f32[4,128,128]{2,0,1:T(4,128)S(1)}, u32[]{:S(2)}, u32[]{:S(2)}) collective-permute-start(f32[4,128,128]{2,0,1:T(4,128)S(1)} %get-tuple-element.248), channel_id=1, source_target_pairs={{0,4},{4,8},{8,12},{12,16},{16,20},{20,24},{24,28},{1,5},{5,9},{9,... | collective-permute-start | bytes 786440 | tf_op jit(solution)/shard_map/ppermute | solution.py:15
  240.1 3.8 collective-permute-done.10
  244.9 64.1 %all-gather.2.cloned.1.call-done = f32[512,512]{1,0:T(8,128)} async-done(((f32[512,128]{1,0:T(8,128)}), f32[512,512]{1,0:T(8,128)}) %all-gather.2.cloned.1.call-update) | async-done | bytes 1048592 | tf_op jit(solution)/shard_map/all_gather | solution.py:92
  308.9 2.8 convolution_multiply_fusion
  311.7 72.2 %all-reduce.2.cloned.1.call-done = f32[128,512]{1,0:T(8,128)} async-done(((f32[128,512]{1,0:T(8,128)}), f32[128,512]{1,0:T(8,128)}) %all-reduce.2.cloned.1.call-update) | async-done | bytes 262160 | tf_op jit(solution)/shard_map/psum | solution.py:102
  (130 shorter events, 72.8 us)
Async XLA Ops:
  7.2 301.8 %all-gather.2.cloned.1.call-start = ((), (), s32[]{:S(2)}) async-start(), calls=%async_computation | async-start | bytes 1310720 | tf_op jit(solution)/shard_map/all_gather | solution.py:92
  7.2 8.2 %copy-start.1 = (s32[64,2]{0,1:T(2,128)S(1)}, s32[64,2]{0,1:T(2,128)}, u32[]{:S(2)}) copy-start(s32[64,2]{0,1:T(2,128)} %param.12) | copy-start | bytes 1540
  7.2 14.9 %collective-permute-start.1 = (f32[4,128,128]{2,1,0:T(8,128)}, f32[4,128,128]{2,1,0:T(8,128)S(1)}, u32[]{:S(2)}, u32[]{:S(2)}) collective-permute-start(f32[4,128,128]{2,1,0:T(8,128)} %bitcast.89), channel_id=1, source_target_pairs={{8,0},{12,4},{16,8},{20,12},{24,16},{28,20},{9,1},{13,5},{17,9},{2... | collective-permute-start | bytes 786440 | tf_op jit(solution)/shard_map/ppermute | solution.py:15
  8.5 13.6 %collective-permute-start = (f32[4,128,128]{2,1,0:T(8,128)}, f32[4,128,128]{2,1,0:T(8,128)S(1)}, u32[]{:S(2)}, u32[]{:S(2)}) collective-permute-start(f32[4,128,128]{2,1,0:T(8,128)} %bitcast.90), channel_id=1, source_target_pairs={{4,0},{8,4},{12,8},{16,12},{20,16},{24,20},{28,24},{5,1},{9,5},{13... | collective-permute-start | bytes 786440 | tf_op jit(solution)/shard_map/ppermute | solution.py:15
  15.4 6.7 %copy-start = (f32[512,128]{1,0:T(8,128)S(1)}, f32[512,128]{1,0:T(8,128)}, u32[]{:S(2)}) copy-start(f32[512,128]{1,0:T(8,128)} %param.10) | copy-start | bytes 786436
  46.9 7.8 %collective-permute-start.3 = (f32[4,128,128]{2,0,1:T(4,128)S(1)}, f32[4,128,128]{2,0,1:T(4,128)S(1)}, u32[]{:S(2)}, u32[]{:S(2)}) collective-permute-start(f32[4,128,128]{2,0,1:T(4,128)S(1)} %get-tuple-element.253), channel_id=1, source_target_pairs={{0,8},{4,12},{8,16},{12,20},{16,24},{20,28},{1,9},{5,13},{9,17},{1... | collective-permute-start | bytes 786440 | tf_op jit(solution)/shard_map/ppermute | solution.py:15
  48.2 11.1 %collective-permute-start.2 = (f32[4,128,128]{2,0,1:T(4,128)S(1)}, f32[4,128,128]{2,0,1:T(4,128)S(1)}, u32[]{:S(2)}, u32[]{:S(2)}) collective-permute-start(f32[4,128,128]{2,0,1:T(4,128)S(1)} %get-tuple-element.252), channel_id=1, source_target_pairs={{0,4},{4,8},{8,12},{12,16},{16,20},{20,24},{24,28},{1,5},{5,9},{9,... | collective-permute-start | bytes 786440 | tf_op jit(solution)/shard_map/ppermute | solution.py:15
  59.5 54.4 %collective-permute-start.5 = (f32[4,128,128]{2,1,0:T(8,128)S(1)}, f32[4,128,128]{2,1,0:T(8,128)S(1)}, u32[]{:S(2)}, u32[]{:S(2)}) collective-permute-start(f32[4,128,128]{2,1,0:T(8,128)S(1)} %bitcast.83), channel_id=1, source_target_pairs={{8,0},{12,4},{16,8},{20,12},{24,16},{28,20},{9,1},{13,5},{17,9},{2... | collective-permute-start | bytes 786440 | tf_op jit(solution)/shard_map/ppermute | solution.py:15
  60.8 53.1 %collective-permute-start.4 = (f32[4,128,128]{2,1,0:T(8,128)S(1)}, f32[4,128,128]{2,1,0:T(8,128)S(1)}, u32[]{:S(2)}, u32[]{:S(2)}) collective-permute-start(f32[4,128,128]{2,1,0:T(8,128)S(1)} %bitcast.84), channel_id=1, source_target_pairs={{4,0},{8,4},{12,8},{16,12},{20,16},{24,20},{28,24},{5,1},{9,5},{13... | collective-permute-start | bytes 786440 | tf_op jit(solution)/shard_map/ppermute | solution.py:15
  138.7 7.8 %collective-permute-start.7 = (f32[4,128,128]{2,0,1:T(4,128)S(1)}, f32[4,128,128]{2,0,1:T(4,128)S(1)}, u32[]{:S(2)}, u32[]{:S(2)}) collective-permute-start(f32[4,128,128]{2,0,1:T(4,128)S(1)} %get-tuple-element.251), channel_id=1, source_target_pairs={{0,8},{4,12},{8,16},{12,20},{16,24},{20,28},{1,9},{5,13},{9,17},{1... | collective-permute-start | bytes 786440 | tf_op jit(solution)/shard_map/ppermute | solution.py:15
  140.0 10.3 %collective-permute-start.6 = (f32[4,128,128]{2,0,1:T(4,128)S(1)}, f32[4,128,128]{2,0,1:T(4,128)S(1)}, u32[]{:S(2)}, u32[]{:S(2)}) collective-permute-start(f32[4,128,128]{2,0,1:T(4,128)S(1)} %get-tuple-element.250), channel_id=1, source_target_pairs={{0,4},{4,8},{8,12},{12,16},{16,20},{20,24},{24,28},{1,5},{5,9},{9,... | collective-permute-start | bytes 786440 | tf_op jit(solution)/shard_map/ppermute | solution.py:15
  150.6 57.0 %collective-permute-start.9 = (f32[4,128,128]{2,1,0:T(8,128)S(1)}, f32[4,128,128]{2,1,0:T(8,128)S(1)}, u32[]{:S(2)}, u32[]{:S(2)}) collective-permute-start(f32[4,128,128]{2,1,0:T(8,128)S(1)} %bitcast.95), channel_id=1, source_target_pairs={{8,0},{12,4},{16,8},{20,12},{24,16},{28,20},{9,1},{13,5},{17,9},{2... | collective-permute-start | bytes 786440 | tf_op jit(solution)/shard_map/ppermute | solution.py:15
  151.9 55.7 %collective-permute-start.8 = (f32[4,128,128]{2,1,0:T(8,128)S(1)}, f32[4,128,128]{2,1,0:T(8,128)S(1)}, u32[]{:S(2)}, u32[]{:S(2)}) collective-permute-start(f32[4,128,128]{2,1,0:T(8,128)S(1)} %bitcast.96), channel_id=1, source_target_pairs={{4,0},{8,4},{12,8},{16,12},{20,16},{24,20},{28,24},{5,1},{9,5},{13... | collective-permute-start | bytes 786440 | tf_op jit(solution)/shard_map/ppermute | solution.py:15
  232.5 7.5 %collective-permute-start.11 = (f32[4,128,128]{2,0,1:T(4,128)S(1)}, f32[4,128,128]{2,0,1:T(4,128)S(1)}, u32[]{:S(2)}, u32[]{:S(2)}) collective-permute-start(f32[4,128,128]{2,0,1:T(4,128)S(1)} %get-tuple-element.249), channel_id=1, source_target_pairs={{0,8},{4,12},{8,16},{12,20},{16,24},{20,28},{1,9},{5,13},{9,17},{1... | collective-permute-start | bytes 786440 | tf_op jit(solution)/shard_map/ppermute | solution.py:15
  233.9 10.1 %collective-permute-start.10 = (f32[4,128,128]{2,0,1:T(4,128)S(1)}, f32[4,128,128]{2,0,1:T(4,128)S(1)}, u32[]{:S(2)}, u32[]{:S(2)}) collective-permute-start(f32[4,128,128]{2,0,1:T(4,128)S(1)} %get-tuple-element.248), channel_id=1, source_target_pairs={{0,4},{4,8},{8,12},{12,16},{16,20},{20,24},{24,28},{1,5},{5,9},{9,... | collective-permute-start | bytes 786440 | tf_op jit(solution)/shard_map/ppermute | solution.py:15
  244.8 139.1 %all-reduce.2.cloned.1.call-start = ((), (), s32[]{:S(2)}) async-start(), calls=%async_computation.1 | async-start | bytes 524288 | tf_op jit(solution)/shard_map/psum | solution.py:102
Sparse Core Ops, SparseCore 0:
  244.9 63.9 all-gather.1
  312.8 71.0 all-reduce.1
where the time goes:
time: 395 us; the launch traced here: 392 us
  waiting for transfers between devices  256 us (65%)
  matrix products  58.6 us (15%)
  starting transfers between devices  30 us (8%)
  local copies, waits for them, and re-layouts  18.4 us (5%)
  between operations  15 us (4%)
  other arithmetic  14 us (4%)
    ppermute x12, waiting for transfers between devices, from_behind(): return lax.ppermute(block, axis, route)  119 us
    psum x1, waiting for transfers between devices, shards(): gram = lax.psum(partial_block, 'domain')  72.2 us
    all_gather x1, waiting for transfers between devices, shards(): gathered = lax.all_gather(filtered, 'vec', axis=1, tiled=True)  64.1 us
    ppermute x12, starting transfers between devices, from_behind(): return lax.ppermute(block, axis, route)  29.9 us
    dot_general x9, matrix products, block_step(): jnp.einsum('tji,tjc->tic', tile, own[rloc], precision=lax.Precision.HIGHEST)  18.5 us
    dot_general x9, matrix products, block_step(): jnp.einsum('tij,tjc->tic', tile, window[cloc], precision=lax.Precision.HI...  15.2 us
    dot_general x9, matrix products, block_step(): jnp.einsum('tg,tic->gic', col_hot, back, precision=lax.Precision.HIGHEST)  13.5 us
    dot_general x9, matrix products, block_step(): jnp.einsum('tg,tic->gic', row_hot, fwd, precision=lax.Precision.HIGHEST)  8.57 us
  transfers between devices with their start and end apart: 14, of which 8 were waited for; matrix products, arithmetic and copies ran while one was open for 3% of the time, Pallas kernels for 0%

commit v1 on v0

--- a/solution.py
+++ b/solution.py
@@ -99,7 +99,9 @@
         )
         / total_rows
     )
-    gram = lax.psum(partial_block, "domain")
+    gram = partial_block
+    for hop in (1, 2, 4):
+        gram = gram + lax.ppermute(gram, "domain", [(dev, dev ^ hop) for dev in range(8)])
     return (filtered, gram)
 
 

time: 395 us -> 351 us (0.89)
  waiting for transfers between devices: 256 us -> 207 us
  starting transfers between devices: 30 us -> 35.5 us
    psum x1 -> x0, waiting for transfers between devices: 72.2 us -> none  [shards(): gram = lax.psum(partial_block, 'domain')]
    ppermute x0 -> x3, waiting for transfers between devices: none -> 23.9 us  [shards(): lax.ppermute(gram, 'domain', [(dev, dev ^ hop) for dev in range(8)])]
    ppermute x0 -> x3, starting transfers between devices: none -> 5.56 us  [shards(): lax.ppermute(gram, 'domain', [(dev, dev ^ hop) for dev in range(8)])]
  transfers between devices with their start and end apart: 14 -> 16, of which waited for: 8 -> 10; matrix products, arithmetic and copies ran while one was open for 3% -> 3% of each run, Pallas kernels for 0% -> 0%
where the time goes in v1:
time: 351 us; the launch traced here: 348 us
  waiting for transfers between devices  207 us (59%)
  matrix products  57.9 us (16%)
  starting transfers between devices  35.5 us (10%)
  local copies, waits for them, and re-layouts  16.8 us (5%)
  between operations  15 us (4%)
  other arithmetic  14.8 us (4%)
    ppermute x12, waiting for transfers between devices, from_behind(): return lax.ppermute(block, axis, route)  119 us
    all_gather x1, waiting for transfers between devices, shards(): gathered = lax.all_gather(filtered, 'vec', axis=1, tiled=True)  64.1 us
    ppermute x12, starting transfers between devices, from_behind(): return lax.ppermute(block, axis, route)  29.9 us
    ppermute x3, waiting for transfers between devices, shards(): lax.ppermute(gram, 'domain', [(dev, dev ^ hop) for dev in range(8)])  23.9 us
    dot_general x9, matrix products, block_step(): jnp.einsum('tji,tjc->tic', tile, own[rloc], precision=lax.Precision.HIGHEST)  18.5 us
    dot_general x9, matrix products, block_step(): jnp.einsum('tij,tjc->tic', tile, window[cloc], precision=lax.Precision.HI...  15.2 us
    dot_general x9, matrix products, block_step(): jnp.einsum('tg,tic->gic', col_hot, back, precision=lax.Precision.HIGHEST)  13.5 us
    dot_general x9, matrix products, block_step(): jnp.einsum('tg,tic->gic', row_hot, fwd, precision=lax.Precision.HIGHEST)  8.57 us
  transfers between devices with their start and end apart: 16, of which 10 were waited for; matrix products, arithmetic and copies ran while one was open for 3% of the time, Pallas kernels for 0%

profile of v1, /device:TPU:0, one launch (start us, length us, event | category | flops | bytes accessed | tf_op | source)
XLA Modules:
  0.0 348.2 jit_solution(14744054179005626905)
XLA Ops:
  9.8 5.6 %copy.6 = f32[64,128,128]{1,2,0:T(8,128)} copy(f32[64,128,128]{2,1,0:T(8,128)} %param.11) | data formatting | bytes 8388608 | tf_op args[1]
  15.5 6.0 %fusion.61 = f32[64,128,128]{2,1,0:T(8,128)} fusion(f32[64,128,128]{2,1,0:T(8,128)} %param.11, f32[64,128,128]{1,2,0:T(8,128)} %copy.6, pred[64]{0:T(512)(128)(4,1)S(1)} %compare_bitcast_fusion), kind=kLoop, calls=%fused_computation.98 | loop fusion | flops 3145728 | bytes 12582976 | tf_op jit(solution)/shard_map/jit(_where)/select_n | solution.py:73
  22.3 24.5 %while.36 = (s32[]{:T(128)}, f32[4,128,128]{2,0,1:T(4,128)S(1)}, f32[12,128,128]{2,0,1:T(8,128)S(1)}, s32[]{:T(128)}, s32[64]{0:T(128)S(1)}, /*index=5*/s32[]{:T...) while((s32[]{:T(128)}, f32[4,128,128]{2,0,1:T(4,128)S(1)}, ...), condition=%wide.region_1.2_spmd, body=%wide.region_0.1_spmd.sunk | while | flops 428083552 | bytes 8397583 | solution.py:50
  26.9 2.1 fusion.117
  35.1 2.1 fusion.117
  43.3 2.1 fusion.117
  48.3 5.6 %collective-permute-start.2 = (f32[4,128,128]{2,0,1:T(4,128)S(1)}, f32[4,128,128]{2,0,1:T(4,128)S(1)}, u32[]{:S(2)}, u32[]{:S(2)}) collective-permute-start(f32[4,128,128]{2,0,1:T(4,128)S(1)} %get-tuple-element.252), channel_id=1, source_target_pairs={{0,4},{4,8},{8,12},{12,16},{16,20},{20,24},{24,28},{1,5},{5,9},{9,... | collective-permute-start | bytes 786440 | tf_op jit(solution)/shard_map/ppermute | solution.py:15
  54.7 4.6 %collective-permute-done.2 = f32[4,128,128]{2,0,1:T(4,128)S(1)} collective-permute-done((f32[4,128,128]{2,0,1:T(4,128)S(1)}, f32[4,128,128]{2,0,1:T(4,128)S(1)}, u32[]{:S(2)}, u32[]{:S(2)}) %collective-permute-start.2) | collective-permute-done | bytes 262176 | tf_op jit(solution)/shard_map/ppermute | solution.py:15
  62.1 51.8 %collective-permute-done.5 = f32[4,128,128]{2,1,0:T(8,128)S(1)} collective-permute-done((f32[4,128,128]{2,1,0:T(8,128)S(1)}, f32[4,128,128]{2,1,0:T(8,128)S(1)}, u32[]{:S(2)}, u32[]{:S(2)}) %collective-permute-start.5) | collective-permute-done | bytes 262176 | tf_op jit(solution)/shard_map/ppermute | solution.py:15
  114.1 24.5 %while.37 = (s32[]{:T(128)}, f32[4,128,128]{2,0,1:T(4,128)S(1)}, f32[12,128,128]{2,0,1:T(8,128)S(1)}, s32[]{:T(128)}, s32[64]{0:T(128)S(1)}, /*index=5*/s32[]{:T...) while((s32[]{:T(128)}, f32[4,128,128]{2,0,1:T(4,128)S(1)}, ...), condition=%wide.region_3.4_spmd, body=%wide.region_2.3_spmd.sunk | while | flops 428083552 | bytes 8397583 | solution.py:50
  135.1 2.1 fusion.127
  140.1 6.4 %collective-permute-start.6 = (f32[4,128,128]{2,0,1:T(4,128)S(1)}, f32[4,128,128]{2,0,1:T(4,128)S(1)}, u32[]{:S(2)}, u32[]{:S(2)}) collective-permute-start(f32[4,128,128]{2,0,1:T(4,128)S(1)} %get-tuple-element.250), channel_id=1, source_target_pairs={{0,4},{4,8},{8,12},{12,16},{16,20},{20,24},{24,28},{1,5},{5,9},{9,... | collective-permute-start | bytes 786440 | tf_op jit(solution)/shard_map/ppermute | solution.py:15
  146.5 3.8 %collective-permute-done.6 = f32[4,128,128]{2,0,1:T(4,128)S(1)} collective-permute-done((f32[4,128,128]{2,0,1:T(4,128)S(1)}, f32[4,128,128]{2,0,1:T(4,128)S(1)}, u32[]{:S(2)}, u32[]{:S(2)}) %collective-permute-start.6) | collective-permute-done | bytes 262176 | tf_op jit(solution)/shard_map/ppermute | solution.py:15
  153.2 54.4 %collective-permute-done.9 = f32[4,128,128]{2,1,0:T(8,128)S(1)} collective-permute-done((f32[4,128,128]{2,1,0:T(8,128)S(1)}, f32[4,128,128]{2,1,0:T(8,128)S(1)}, u32[]{:S(2)}, u32[]{:S(2)}) %collective-permute-start.9) | collective-permute-done | bytes 262176 | tf_op jit(solution)/shard_map/ppermute | solution.py:15
  207.7 24.7 %while.38 = (s32[]{:T(128)}, f32[4,128,128]{2,0,1:T(4,128)S(1)}, f32[12,128,128]{2,0,1:T(8,128)S(1)}, s32[]{:T(128)}, s32[64]{0:T(128)S(1)}, /*index=5*/s32[]{:T...) while((s32[]{:T(128)}, f32[4,128,128]{2,0,1:T(4,128)S(1)}, ...), condition=%wide.region_5.6_spmd, body=%wide.region_4.5_spmd.sunk | while | flops 428083552 | bytes 8397583 | solution.py:50
  212.5 2.1 fusion.137
  233.9 6.2 %collective-permute-start.10 = (f32[4,128,128]{2,0,1:T(4,128)S(1)}, f32[4,128,128]{2,0,1:T(4,128)S(1)}, u32[]{:S(2)}, u32[]{:S(2)}) collective-permute-start(f32[4,128,128]{2,0,1:T(4,128)S(1)} %get-tuple-element.248), channel_id=1, source_target_pairs={{0,4},{4,8},{8,12},{12,16},{16,20},{20,24},{24,28},{1,5},{5,9},{9,... | collective-permute-start | bytes 786440 | tf_op jit(solution)/shard_map/ppermute | solution.py:15
  240.1 3.8 %collective-permute-done.10 = f32[4,128,128]{2,0,1:T(4,128)S(1)} collective-permute-done((f32[4,128,128]{2,0,1:T(4,128)S(1)}, f32[4,128,128]{2,0,1:T(4,128)S(1)}, u32[]{:S(2)}, u32[]{:S(2)}) %collective-permute-start.10) | collective-permute-done | bytes 262176 | tf_op jit(solution)/shard_map/ppermute | solution.py:15
  244.8 64.1 %all-gather.2.cloned.1.call-done = f32[512,512]{1,0:T(8,128)} async-done(((f32[512,128]{1,0:T(8,128)}), f32[512,512]{1,0:T(8,128)}) %all-gather.2.cloned.1.call-update) | async-done | bytes 1048592 | tf_op jit(solution)/shard_map/all_gather | solution.py:92
  308.9 2.1 convolution_multiply_fusion
  312.6 7.0 %collective-permute-done.12 = f32[128,512]{1,0:T(8,128)S(1)} collective-permute-done((f32[128,512]{1,0:T(8,128)S(1)}, f32[128,512]{1,0:T(8,128)S(1)}, u32[]{:S(2)}, u32[]{:S(2)}) %collective-permute-start.12) | collective-permute-done | bytes 262176 | tf_op jit(solution)/shard_map/ppermute | solution.py:104
  321.1 6.1 %collective-permute-done.13 = f32[128,512]{1,0:T(8,128)S(1)} collective-permute-done((f32[128,512]{1,0:T(8,128)S(1)}, f32[128,512]{1,0:T(8,128)S(1)}, u32[]{:S(2)}, u32[]{:S(2)}) %collective-permute-start.13) | collective-permute-done | bytes 262176 | tf_op jit(solution)/shard_map/ppermute | solution.py:104
  327.3 2.5 collective-permute-start.14
  329.7 10.8 %collective-permute-done.14 = f32[128,512]{1,0:T(8,128)S(1)} collective-permute-done((f32[128,512]{1,0:T(8,128)S(1)}, f32[128,512]{1,0:T(8,128)S(1)}, u32[]{:S(2)}, u32[]{:S(2)}) %collective-permute-start.14) | collective-permute-done | bytes 262176 | tf_op jit(solution)/shard_map/ppermute | solution.py:104
  (135 shorter events, 81.2 us)
Async XLA Ops:
  7.2 301.8 %all-gather.2.cloned.1.call-start = ((), (), s32[]{:S(2)}) async-start(), calls=%async_computation | async-start | bytes 1310720 | tf_op jit(solution)/shard_map/all_gather | solution.py:92
  7.2 8.2 %copy-start.1 = (s32[64,2]{0,1:T(2,128)S(1)}, s32[64,2]{0,1:T(2,128)}, u32[]{:S(2)}) copy-start(s32[64,2]{0,1:T(2,128)} %param.12) | copy-start | bytes 1540
  7.2 14.9 %collective-permute-start.1 = (f32[4,128,128]{2,1,0:T(8,128)}, f32[4,128,128]{2,1,0:T(8,128)S(1)}, u32[]{:S(2)}, u32[]{:S(2)}) collective-permute-start(f32[4,128,128]{2,1,0:T(8,128)} %bitcast.89), channel_id=1, source_target_pairs={{8,0},{12,4},{16,8},{20,12},{24,16},{28,20},{9,1},{13,5},{17,9},{2... | collective-permute-start | bytes 786440 | tf_op jit(solution)/shard_map/ppermute | solution.py:15
  8.5 13.6 %collective-permute-start = (f32[4,128,128]{2,1,0:T(8,128)}, f32[4,128,128]{2,1,0:T(8,128)S(1)}, u32[]{:S(2)}, u32[]{:S(2)}) collective-permute-start(f32[4,128,128]{2,1,0:T(8,128)} %bitcast.90), channel_id=1, source_target_pairs={{4,0},{8,4},{12,8},{16,12},{20,16},{24,20},{28,24},{5,1},{9,5},{13... | collective-permute-start | bytes 786440 | tf_op jit(solution)/shard_map/ppermute | solution.py:15
  15.4 6.7 %copy-start = (f32[512,128]{1,0:T(8,128)S(1)}, f32[512,128]{1,0:T(8,128)}, u32[]{:S(2)}) copy-start(f32[512,128]{1,0:T(8,128)} %param.10) | copy-start | bytes 786436
  46.9 7.8 %collective-permute-start.3 = (f32[4,128,128]{2,0,1:T(4,128)S(1)}, f32[4,128,128]{2,0,1:T(4,128)S(1)}, u32[]{:S(2)}, u32[]{:S(2)}) collective-permute-start(f32[4,128,128]{2,0,1:T(4,128)S(1)} %get-tuple-element.253), channel_id=1, source_target_pairs={{0,8},{4,12},{8,16},{12,20},{16,24},{20,28},{1,9},{5,13},{9,17},{1... | collective-permute-start | bytes 786440 | tf_op jit(solution)/shard_map/ppermute | solution.py:15
  48.3 11.1 %collective-permute-start.2 = (f32[4,128,128]{2,0,1:T(4,128)S(1)}, f32[4,128,128]{2,0,1:T(4,128)S(1)}, u32[]{:S(2)}, u32[]{:S(2)}) collective-permute-start(f32[4,128,128]{2,0,1:T(4,128)S(1)} %get-tuple-element.252), channel_id=1, source_target_pairs={{0,4},{4,8},{8,12},{12,16},{16,20},{20,24},{24,28},{1,5},{5,9},{9,... | collective-permute-start | bytes 786440 | tf_op jit(solution)/shard_map/ppermute | solution.py:15
  59.5 54.4 %collective-permute-start.5 = (f32[4,128,128]{2,1,0:T(8,128)S(1)}, f32[4,128,128]{2,1,0:T(8,128)S(1)}, u32[]{:S(2)}, u32[]{:S(2)}) collective-permute-start(f32[4,128,128]{2,1,0:T(8,128)S(1)} %bitcast.83), channel_id=1, source_target_pairs={{8,0},{12,4},{16,8},{20,12},{24,16},{28,20},{9,1},{13,5},{17,9},{2... | collective-permute-start | bytes 786440 | tf_op jit(solution)/shard_map/ppermute | solution.py:15
  60.8 53.1 %collective-permute-start.4 = (f32[4,128,128]{2,1,0:T(8,128)S(1)}, f32[4,128,128]{2,1,0:T(8,128)S(1)}, u32[]{:S(2)}, u32[]{:S(2)}) collective-permute-start(f32[4,128,128]{2,1,0:T(8,128)S(1)} %bitcast.84), channel_id=1, source_target_pairs={{4,0},{8,4},{12,8},{16,12},{20,16},{24,20},{28,24},{5,1},{9,5},{13... | collective-permute-start | bytes 786440 | tf_op jit(solution)/shard_map/ppermute | solution.py:15
  138.7 7.8 %collective-permute-start.7 = (f32[4,128,128]{2,0,1:T(4,128)S(1)}, f32[4,128,128]{2,0,1:T(4,128)S(1)}, u32[]{:S(2)}, u32[]{:S(2)}) collective-permute-start(f32[4,128,128]{2,0,1:T(4,128)S(1)} %get-tuple-element.251), channel_id=1, source_target_pairs={{0,8},{4,12},{8,16},{12,20},{16,24},{20,28},{1,9},{5,13},{9,17},{1... | collective-permute-start | bytes 786440 | tf_op jit(solution)/shard_map/ppermute | solution.py:15
  140.1 10.3 %collective-permute-start.6 = (f32[4,128,128]{2,0,1:T(4,128)S(1)}, f32[4,128,128]{2,0,1:T(4,128)S(1)}, u32[]{:S(2)}, u32[]{:S(2)}) collective-permute-start(f32[4,128,128]{2,0,1:T(4,128)S(1)} %get-tuple-element.250), channel_id=1, source_target_pairs={{0,4},{4,8},{8,12},{12,16},{16,20},{20,24},{24,28},{1,5},{5,9},{9,... | collective-permute-start | bytes 786440 | tf_op jit(solution)/shard_map/ppermute | solution.py:15
  150.6 57.0 %collective-permute-start.9 = (f32[4,128,128]{2,1,0:T(8,128)S(1)}, f32[4,128,128]{2,1,0:T(8,128)S(1)}, u32[]{:S(2)}, u32[]{:S(2)}) collective-permute-start(f32[4,128,128]{2,1,0:T(8,128)S(1)} %bitcast.95), channel_id=1, source_target_pairs={{8,0},{12,4},{16,8},{20,12},{24,16},{28,20},{9,1},{13,5},{17,9},{2... | collective-permute-start | bytes 786440 | tf_op jit(solution)/shard_map/ppermute | solution.py:15
  151.9 55.7 %collective-permute-start.8 = (f32[4,128,128]{2,1,0:T(8,128)S(1)}, f32[4,128,128]{2,1,0:T(8,128)S(1)}, u32[]{:S(2)}, u32[]{:S(2)}) collective-permute-start(f32[4,128,128]{2,1,0:T(8,128)S(1)} %bitcast.96), channel_id=1, source_target_pairs={{4,0},{8,4},{12,8},{16,12},{20,16},{24,20},{28,24},{5,1},{9,5},{13... | collective-permute-start | bytes 786440 | tf_op jit(solution)/shard_map/ppermute | solution.py:15
  232.6 7.5 %collective-permute-start.11 = (f32[4,128,128]{2,0,1:T(4,128)S(1)}, f32[4,128,128]{2,0,1:T(4,128)S(1)}, u32[]{:S(2)}, u32[]{:S(2)}) collective-permute-start(f32[4,128,128]{2,0,1:T(4,128)S(1)} %get-tuple-element.249), channel_id=1, source_target_pairs={{0,8},{4,12},{8,16},{12,20},{16,24},{20,28},{1,9},{5,13},{9,17},{1... | collective-permute-start | bytes 786440 | tf_op jit(solution)/shard_map/ppermute | solution.py:15
  233.9 10.1 %collective-permute-start.10 = (f32[4,128,128]{2,0,1:T(4,128)S(1)}, f32[4,128,128]{2,0,1:T(4,128)S(1)}, u32[]{:S(2)}, u32[]{:S(2)}) collective-permute-start(f32[4,128,128]{2,0,1:T(4,128)S(1)} %get-tuple-element.248), channel_id=1, source_target_pairs={{0,4},{4,8},{8,12},{12,16},{16,20},{20,24},{24,28},{1,5},{5,9},{9,... | collective-permute-start | bytes 786440 | tf_op jit(solution)/shard_map/ppermute | solution.py:15
  311.0 8.5 %collective-permute-start.12 = (f32[128,512]{1,0:T(8,128)S(1)}, f32[128,512]{1,0:T(8,128)S(1)}, u32[]{:S(2)}, u32[]{:S(2)}) collective-permute-start(f32[128,512]{1,0:T(8,128)S(1)} %convolution_multiply_fusion), channel_id=1, source_target_pairs={{0,4},{4,0},{8,12},{12,8},{16,20},{20,16},{24,28},{28,24},{1,5},{5... | collective-permute-start | bytes 786440 | tf_op jit(solution)/shard_map/ppermute | solution.py:104
  319.6 7.7 %collective-permute-start.13 = (f32[128,512]{1,0:T(8,128)S(1)}, f32[128,512]{1,0:T(8,128)S(1)}, u32[]{:S(2)}, u32[]{:S(2)}) collective-permute-start(f32[128,512]{1,0:T(8,128)S(1)} %add.146), channel_id=1, source_target_pairs={{0,8},{4,12},{8,0},{12,4},{16,24},{20,28},{24,16},{28,20},{1,9},{5... | collective-permute-start | bytes 786440 | tf_op jit(solution)/shard_map/ppermute | solution.py:104
  327.3 13.3 %collective-permute-start.14 = (f32[128,512]{1,0:T(8,128)S(1)}, f32[128,512]{1,0:T(8,128)S(1)}, u32[]{:S(2)}, u32[]{:S(2)}) collective-permute-start(f32[128,512]{1,0:T(8,128)S(1)} %add.147), channel_id=1, source_target_pairs={{0,16},{4,20},{8,24},{12,28},{16,0},{20,4},{24,8},{28,12},{1,17},{... | collective-permute-start | bytes 786440 | tf_op jit(solution)/shard_map/ppermute | solution.py:104
Sparse Core Ops, SparseCore 0:
  244.9 63.9 all-gather.1
